TPU v7x, 32 devices: a whole 2x2x4 slice. The times are simulated.
32 devices in a mesh: tok: 8 (over z, x), tp: 4 (over y, core).
Axes of the slice: x: 2, y: 2, z: 4, core: 2. Of those that a mesh axis runs over, the one named last changes fastest.
Arguments:
- tokens: bfloat16 [36928, 768], P('tok'), may hold values from -6 to 6
- slot_index: int32 [36928], P('tok'), may hold values from -1 to 18477, as said below
- segment: int32 [36928], P('tok'), may hold values from 0 to 3, as said below
- router: float32 [768], replicated, may hold values from -0.21875 to 0.21875
- first_norm: float32 [2, 768], replicated, may hold values from -0.6 to 1.3
- qkv_weight: bfloat16 [768, 3, 768], P(None, None, 'tp'), may hold values from -0.21875 to 0.21875
- qv_bias: float32 [2, 768], P(None, 'tp'), may hold values from -4 to 4
- out_weight: bfloat16 [768, 768], P('tp'), may hold values from -1.75 to 1.75
- out_bias: float32 [768], P('tp'), may hold values from -4 to 4
- second_norm: float32 [2, 768], replicated, may hold values from -0.6 to 1.3
- up_weight: bfloat16 [768, 3072], P(None, 'tp'), may hold values from -0.21875 to 0.21875
- up_bias: float32 [3072], P('tp'), may hold values from -4 to 4
- down_weight: bfloat16 [3072, 768], P('tp'), may hold values from -0.109375 to 0.109375
- down_bias: float32 [768], P('tp'), may hold values from -4 to 4
- cotangent: bfloat16 [36928, 768], P('tok'), may hold values from -6 to 6
Outputs:
- layer_out: bfloat16 [36928, 768], P('tok', 'tp')
- d_tokens: float32 [36928, 768], P('tok', 'tp')
- d_qkv_weight: float32 [768, 3, 768], P(None, None, 'tp')
- d_qv_bias: float32 [2, 768], P(None, 'tp')
- d_out_weight: float32 [768, 768], P('tp')
- d_out_bias: float32 [768], P('tp')
- d_up_weight: float32 [768, 3072], P(None, 'tp')
- d_up_bias: float32 [3072], P('tp')
- d_down_weight: float32 [3072, 768], P('tp')
- d_down_bias: float32 [768], P('tp')
- d_first_norm: float32 [2, 768], P(None, 'tp')
- d_second_norm: float32 [2, 768], P(None, 'tp')
- d_router: float32 [768], P('tp')
Inputs may be any that keep to these rules, and one draw needn't show every extreme that they name: `slot_index`: -1 where the router leaves a patch out; else a slot of the compact buffers, slot // 289 being its row buffer, owned by index slot // 2312 of tok. No slot is named twice, each buffer's named slots are its lowest ones, every index of tok holds exactly 2168 selected patches and owns 2168 named slots, and at most 271 of the selected patches of one index of tok lie in rows of one owner. `segment`: within a row buffer the segments of named slots never fall from one slot to the next.
All inputs are finite; a program needn't handle non-finite values.
Results may differ from a plain program's by a relative error of at most 0.013.
Values may be sent and summed in bfloat16 or wider, within the bound.
No kernel may reach another device: no remote copies, remote signals or barrier semaphores. Data moves between devices by JAX's collectives and lax.ppermute only.
A program may use at most 320 MiB of HBM per device.

v0:
```python
import jax
import jax.numpy as jnp
from jax import lax
from jax.sharding import PartitionSpec as P

HD = 64
ROWS_DEV = 8
SLOTS = 289
EPSILON = 1e-06
MASKED_SCORE = -1000000000.0
BF = jnp.bfloat16
F32 = jnp.float32
EXACT = lax.Precision.HIGHEST


def ceil_to(value, step):
    return -(-value // step) * step


def normal_parts(values):
    row_mean = jnp.mean(values, axis=-1, keepdims=True)
    centered = values - row_mean
    inverse = lax.rsqrt(jnp.mean(centered * centered, axis=-1, keepdims=True) + EPSILON)
    return (centered * inverse, inverse)


def norm_back(grad_in, normal, inverse, gain_row):
    scaled = grad_in * gain_row
    return inverse * (
        scaled
        - jnp.mean(scaled, axis=-1, keepdims=True)
        - normal * jnp.mean(scaled * normal, axis=-1, keepdims=True)
    )


def mul(left, right):
    return lax.dot_general(left, right, (((1,), (0,)), ((), ())), preferred_element_type=F32)


def mul_t0(left, right):
    return lax.dot_general(left, right, (((0,), (0,)), ((), ())), preferred_element_type=F32)


def mul_t1(left, right):
    return lax.dot_general(left, right, (((1,), (1,)), ((), ())), preferred_element_type=F32)


def hot(rows, cols):
    return (rows[:, None] == cols[None, :]).astype(BF)


def columns_of(source, part, shares):
    width = source.shape[-1] // shares
    return lax.dynamic_slice_in_dim(source, part * width, width, source.ndim - 1)


def body(
    tokens,
    slot_index,
    segment,
    router,
    first_norm,
    qkv_weight,
    qv_bias,
    out_weight,
    out_bias,
    second_norm,
    up_weight,
    up_bias,
    down_weight,
    down_bias,
    cotangent,
):
    peers = lax.axis_size("tok")
    shares = lax.axis_size("tp")
    part = lax.axis_index("tp")
    half_bit = part % 2
    pair_bit = part // 2
    half_swap = [(i, i ^ 1) for i in range(shares)]
    pair_swap = [(i, i ^ 2) for i in range(shares)]
    count, width = tokens.shape
    inner = qkv_weight.shape[2]
    heads_local = inner // HD
    owned = ROWS_DEV * SLOTS
    live = owned - owned // 16
    capacity = -(-live // peers)
    quarter = -(-capacity // shares)
    block = ceil_to(quarter + 1, 8)
    picked = peers * block
    idle_share = -(-(count - live) // shares)
    idle = ceil_to(idle_share, 16)
    own = picked + idle
    chosen = slot_index >= 0
    owner = jnp.where(chosen, slot_index // owned, peers)
    lanes = jnp.arange(peers, dtype=jnp.int32)
    match = (owner[:, None] == lanes[None, :]).astype(jnp.int32)
    rank = jnp.sum(jnp.cumsum(match, axis=0) * match, axis=1) - 1
    idle_rank = jnp.cumsum(jnp.where(chosen, 0, 1)) - 1
    piece = rank // quarter
    offset = rank % quarter
    mine = chosen & (piece % 2 == half_bit)
    far = piece // 2 ^ pair_bit
    send_row = jnp.where(mine, (owner * 2 + far) * block + offset, -1)
    picked_row = jnp.where(mine & (far == 0), owner * block + offset, -1)
    own_row = jnp.where(
        chosen,
        picked_row,
        jnp.where(idle_rank // idle_share == part, picked + idle_rank % idle_share, -1),
    )
    back_picked = jnp.where(chosen, piece * picked + owner * block + offset, -1)
    back_idle = jnp.where(chosen, -1, idle_rank // idle_share * idle + idle_rank % idle_share)
    up_all = lax.all_gather(up_weight, "tp")
    down_all = lax.all_gather(down_weight, "tp")
    send_hot = hot(jnp.arange(2 * picked, dtype=jnp.int32), send_row)
    own_hot = hot(jnp.arange(own, dtype=jnp.int32), own_row)
    send_in = mul(send_hot, tokens)
    send_hat, _ = normal_parts(send_in)
    send_rows = (send_hat * first_norm[0] + first_norm[1]).astype(BF)
    local_slot = jnp.where(chosen, slot_index % owned, 0)
    marks = jnp.stack([local_slot // 64 + 1, local_slot % 64, segment])
    block_of = jnp.where(mine, owner * 2 + far, -1)
    block_hot = jnp.arange(2 * peers, dtype=jnp.int32)[:, None] == block_of[None, :]
    mark_left = jnp.where(block_hot[None], marks[:, None, :], 0).astype(BF)
    mark_right = hot(offset, jnp.arange(128, dtype=jnp.int32))
    mark_rows = mul(mark_left.reshape(6 * peers, count), mark_right).astype(BF)
    mark_rows = mark_rows.reshape(3, 2 * peers, 128).transpose(1, 0, 2).reshape(2 * peers, 1, 384)
    mark_rows = jnp.pad(mark_rows, ((0, 0), (0, 0), (0, width - 384)))
    row_kind = jnp.arange(block, dtype=jnp.int32)[None, :, None] == quarter
    send_rows = jnp.where(row_kind, mark_rows, send_rows.reshape(2 * peers, block, width))
    got_near = lax.all_to_all(
        send_rows.reshape(peers, 2, block, width), "tok", split_axis=0, concat_axis=0, tiled=True
    )
    got_far = lax.ppermute(got_near, "tp", half_swap)
    got = jnp.stack([got_near, got_far])
    mark = got[:, :, :, quarter, :].astype(jnp.int32)
    recv_slot = (mark[..., 0:block] - 1) * 64 + mark[..., 128 : 128 + block]
    recv_segment = mark[..., 256 : 256 + block]
    slot_rows = recv_slot.transpose(0, 2, 1, 3).reshape(4 * picked)
    segment_rows = recv_segment.transpose(0, 2, 1, 3).reshape(4 * picked)
    features = got.transpose(0, 2, 1, 3, 4).reshape(4 * picked, width)
    pad = 304
    ids = jnp.arange(ROWS_DEV * pad, dtype=jnp.int32)
    slot_ids = jnp.where(ids % pad < SLOTS, ids // pad * SLOTS + ids % pad, -1000)
    slot_hot = hot(slot_ids, slot_rows)
    slot_features = mul(slot_hot, features).astype(BF)
    flat_weight = qkv_weight.reshape(width, 3 * inner)
    bias_row = jnp.concatenate([qv_bias[0], jnp.zeros_like(qv_bias[0]), qv_bias[1]])
    slot_qkv = (mul(slot_features, flat_weight) + bias_row).astype(BF)
    slot_segment = (
        jnp.sum(jnp.where(slot_hot > 0, segment_rows[None, :] + 1, 0), axis=1) - 1
    ).reshape(ROWS_DEV, pad)
    allowed = (slot_segment[:, :, None] == slot_segment[:, None, :]) & (
        slot_segment[:, None, :] >= 0
    )
    grouped = slot_qkv.reshape(ROWS_DEV, pad, 3, heads_local, HD)
    query, key, value = (grouped[:, :, 0], grouped[:, :, 1], grouped[:, :, 2])
    score_scale = HD ** (-0.5)
    scores = jnp.einsum("rqhe,rkhe->rhqk", query, key, preferred_element_type=F32) * score_scale
    scores = jnp.where(allowed[:, None], scores, MASKED_SCORE)
    top = jnp.max(scores, axis=-1, keepdims=True)
    raised = jnp.exp(scores - top)
    weights = raised / jnp.sum(raised, axis=-1, keepdims=True)
    weights_low = weights.astype(BF)
    attended = jnp.einsum("rhqk,rkhe->rqhe", weights_low, value, preferred_element_type=F32)
    heads = attended.reshape(ROWS_DEV * pad, inner).astype(BF)
    heads_rows = mul_t0(slot_hot, heads).astype(BF)
    bias_full = lax.dynamic_update_slice(
        jnp.zeros((width,), F32), out_bias, (part * (width // shares),)
    )

    def share_sum(partial):
        near, far_half = (partial[: 2 * picked], partial[2 * picked :])
        got_half = lax.ppermute(far_half.astype(BF), "tp", half_swap)
        joined = near + got_half.astype(F32)
        got_pair = lax.ppermute(joined[picked:].astype(BF), "tp", pair_swap)
        return (joined[:picked] + got_pair.astype(F32)).astype(BF)

    def across(rows):
        return lax.all_to_all(
            rows.reshape(peers, block, width), "tok", split_axis=0, concat_axis=0, tiled=True
        ).reshape(picked, width)

    returned = across(share_sum(mul(heads_rows, out_weight) + bias_full))
    own_in = mul(own_hot, tokens)
    own_cot_low = mul(own_hot, cotangent).astype(BF)
    own_cot = own_cot_low.astype(F32)
    gate = jax.nn.sigmoid(jnp.dot(own_in, router, precision=EXACT))
    branch = jnp.pad(returned.astype(F32), ((0, idle), (0, 0)))
    scale = jnp.where(jnp.arange(own) < picked, gate, 0.0)
    residual = own_in + scale[:, None] * branch
    second_hat, second_inv = normal_parts(residual)
    second = (second_hat * second_norm[0] + second_norm[1]).astype(BF)
    up_cols = up_all.transpose(1, 0, 2).reshape(width, -1)
    down_rows = down_all.reshape(-1, width)
    up_bias_all = lax.all_gather(up_bias, "tp", tiled=True)
    down_bias_all = lax.all_gather(down_bias, "tp", tiled=True)
    pre = mul(second, up_cols) + up_bias_all
    below = 0.5 * (1.0 + lax.erf(pre * 2.0 ** (-0.5)))
    bell = jnp.exp(-0.5 * pre * pre) * (2.0 * jnp.pi) ** (-0.5)
    hidden = (pre * below).astype(BF)
    layer_rows = (residual + mul(hidden, down_rows) + down_bias_all).astype(BF)
    d_hidden = mul_t1(own_cot_low, down_rows)
    d_pre = (d_hidden * (below + pre * bell)).astype(BF)
    d_down = mul_t0(hidden, own_cot_low).astype(BF).reshape(shares, -1, width)
    d_up = mul_t0(second, d_pre).astype(BF)
    d_up = d_up.reshape(width, shares, -1).transpose(1, 0, 2)
    d_second = mul_t1(d_pre, up_cols)
    d_residual = own_cot + norm_back(d_second, second_hat, second_inv, second_norm[0])
    d_branch = (d_residual[:picked] * scale[:picked, None]).astype(BF)
    d_logit = jnp.sum(d_residual * branch, axis=1) * scale * (1.0 - gate)
    small = jnp.concatenate(
        [
            jnp.sum(d_pre.astype(F32), axis=0).reshape(shares, width),
            jnp.stack(
                [
                    jnp.sum(d_second * second_hat, axis=0),
                    jnp.sum(d_second, axis=0),
                    jnp.sum(own_cot, axis=0),
                    jnp.sum(d_branch.astype(F32), axis=0),
                    jnp.sum(d_logit[:, None] * own_in, axis=0),
                ]
            ),
        ]
    )
    d_up_share = lax.psum_scatter(d_up, "tp", scatter_dimension=0)
    d_down_share = lax.psum_scatter(d_down, "tp", scatter_dimension=0)
    d_up_total = lax.psum(d_up_share, "tok").astype(F32)
    d_down_total = lax.psum(d_down_share, "tok").astype(F32)
    grad_own = across(d_branch)
    grad_near = jnp.concatenate([grad_own, lax.ppermute(grad_own, "tp", pair_swap)])
    grad_rows = jnp.concatenate([grad_near, lax.ppermute(grad_near, "tp", half_swap)])
    d_out_weight = mul_t0(heads_rows, grad_rows)
    d_heads_rows = mul_t1(grad_rows, out_weight).astype(BF)
    d_heads = mul(slot_hot, d_heads_rows).astype(BF).reshape(ROWS_DEV, pad, heads_local, HD)
    d_weights = jnp.einsum("rqhe,rkhe->rhqk", d_heads, value, preferred_element_type=F32)
    d_value = jnp.einsum("rhqk,rqhe->rkhe", weights_low, d_heads, preferred_element_type=F32)
    d_scores = (
        weights * (d_weights - jnp.sum(weights * d_weights, axis=-1, keepdims=True))
    ).astype(BF)
    d_query = jnp.einsum("rhqk,rkhe->rqhe", d_scores, key, preferred_element_type=F32) * score_scale
    d_key = jnp.einsum("rhqk,rqhe->rkhe", d_scores, query, preferred_element_type=F32) * score_scale
    d_qkv = (
        jnp.stack([d_query, d_key, d_value], axis=2).astype(BF).reshape(ROWS_DEV * pad, 3 * inner)
    )
    d_qkv_weight = mul_t0(slot_features, d_qkv)
    d_qkv_bias = jnp.sum(d_qkv.astype(F32), axis=0).reshape(3, inner)
    d_qv_bias = jnp.stack([d_qkv_bias[0], d_qkv_bias[2]])
    d_qkv_rows = mul_t0(slot_hot, d_qkv).astype(BF)
    d_normed = across(share_sum(mul_t1(d_qkv_rows, flat_weight))).astype(F32)
    d_qkv_total = lax.psum(d_qkv_weight.astype(BF), "tok").astype(F32)
    d_out_total = lax.psum(d_out_weight.astype(BF), "tok").astype(F32)
    first_hat, first_inv = normal_parts(own_in[:picked])
    d_picked = (
        d_residual[:picked]
        + norm_back(d_normed, first_hat, first_inv, first_norm[0])
        + d_logit[:picked, None] * router[None, :]
    ).astype(BF)
    d_idle = d_residual[picked:].astype(BF)

    def to_columns(rows):
        pieces = rows.reshape(rows.shape[0], shares, width // shares).transpose(1, 0, 2)
        return lax.all_to_all(pieces, "tp", split_axis=0, concat_axis=0, tiled=True).reshape(
            shares * rows.shape[0], width // shares
        )

    picked_hot = hot(back_picked, jnp.arange(shares * picked, dtype=jnp.int32))
    idle_hot = hot(back_idle, jnp.arange(shares * idle, dtype=jnp.int32))
    layer_out = (
        mul(picked_hot, to_columns(layer_rows[:picked]))
        + mul(idle_hot, to_columns(layer_rows[picked:]))
    ).astype(BF)
    d_tokens = mul(picked_hot, to_columns(d_picked)) + mul(idle_hot, to_columns(d_idle))
    first_pair = jnp.stack([jnp.sum(d_normed * first_hat, axis=0), jnp.sum(d_normed, axis=0)])
    small = lax.psum(jnp.concatenate([small, first_pair]), ("tok", "tp"))
    small_cols = columns_of(small[shares:], part, shares)
    d_up_bias = lax.dynamic_slice_in_dim(small, part, 1, 0).reshape(width)
    d_qv_bias = lax.psum(d_qv_bias, "tok")
    return (
        layer_out,
        d_tokens,
        d_qkv_total.reshape(width, 3, inner),
        d_qv_bias,
        d_out_total,
        small_cols[3],
        d_up_total,
        d_up_bias,
        d_down_total,
        small_cols[2],
        small_cols[5:7],
        small_cols[0:2],
        small_cols[4],
    )


def solution(mesh):
    return jax.shard_map(
        body,
        mesh=mesh,
        in_specs=(
            P("tok", None),
            P("tok"),
            P("tok"),
            P(),
            P(),
            P(None, None, "tp"),
            P(None, "tp"),
            P("tp", None),
            P("tp"),
            P(),
            P(None, "tp"),
            P("tp"),
            P("tp", None),
            P("tp"),
            P("tok", None),
        ),
        out_specs=(
            P("tok", "tp"),
            P("tok", "tp"),
            P(None, None, "tp"),
            P(None, "tp"),
            P("tp", None),
            P("tp"),
            P(None, "tp"),
            P("tp"),
            P("tp", None),
            P("tp"),
            P(None, "tp"),
            P(None, "tp"),
            P("tp"),
        ),
        check_vma=False,
    )
```

profile of v0, /device:TPU:0, one launch (start us, length us, event | category | flops | bytes accessed | tf_op | source)
XLA Modules:
  0.0 696.7 jit_solution(4545855774942127467)
XLA Ops:
  16.0 14.7 %fusion.135 = (f32[1152]{0:T(1024)S(1)}, f32[1152,768]{1,0:T(8,128)S(1)}) fusion(bf16[4616,768]{1,0:T(8,128)(2,1)} %param.15, s32[4616]{0:T(1024)S(1)} %get-tuple-element.46), kind=kOutput, calls=%fused_computation.269 | convolution fusion | flops 8174084096 | bytes 10652192 | tf_op jit(solution)/shard_map/dot_general | solution.py:37
  32.1 48.4 %all_to_all.40 = bf16[8,2,72,768]{3,2,1,0:T(8,128)(2,1)S(1)} all-to-all(bf16[8,2,72,768]{3,2,1,0:T(8,128)(2,1)S(1)} %broadcast_select_fusion), channel_id=1, replica_groups=mesh['tok'=8,'tp'=4] {'tok'}, dimensions={0} | all-to-all | bytes 3538944 | tf_op jit(solution)/shard_map/all_to_all | solution.py:130
  81.6 2.9 collective-permute-done
  85.6 3.9 pad_maximum_fusion
  89.7 12.9 %fusion.44 = bf16[2432,768]{1,0:T(8,128)(2,1)} fusion(bf16[2304,768]{1,0:T(8,128)(2,1)} %bitcast.217, s32[2304]{0:T(1024)S(1)} %eq.201, s32[2432]{0:T(1024)S(1)} %fusion.120), kind=kOutput, calls=%fused_computation.64 | convolution fusion | flops 8614182912 | bytes 7293440 | tf_op jit(solution)/shard_map/dot_general | solution.py:37
  102.6 3.8 select_reduce_fusion
  106.5 6.2 add_convert_fusion
  112.7 7.5 %reshape.344 = bf16[8,304,3,3,64]{1,0,4,3,2:T(8,128)(2,1)} reshape(bf16[2432,576]{0,1:T(8,128)(2,1)} %add_convert_fusion) | data formatting | bytes 5603328 | tf_op jit(solution)/shard_map/reshape | solution.py:155
  122.3 3.4 fusion.131
  125.7 8.3 %fusion.136 = (f32[8,3,304]{2,1,0:T(4,128)S(1)}, f32[8,3,304,304]{2,3,1,0:T(8,128)}) fusion(pred[8,304,304]{1,2,0:T(8,128)(4,1)} %compare_and_fusion, bf16[8,304,1,3,64]{1,0,4,3,2:T(8,128)(2,1)S(1)} %get-tuple-element.38, bf16[8,304,1,3,64]{1,0,4,3,2:T(8,128)(2,1)S(1)} %get-tuple-element.37), kind=kOutput, calls=%fused_computation.270 | convolution fusion | flops 292774176 | bytes 11508224 | tf_op jit(solution)/shard_map/sub | solution.py:161
  134.0 5.8 fusion.83
  141.4 4.1 fusion.53
  146.7 2.9 copy-done.4
  150.0 3.7 collective-permute-done.1
  153.7 3.3 slice_add_fusion.1
  158.5 15.1 %fusion.16 = f32[1200,768]{1,0:T(8,128)S(1)} fusion(bf16[4616,768]{1,0:T(8,128)(2,1)} %param.15, s32[4616]{0:T(1024)S(1)} %get-tuple-element.47), kind=kOutput, calls=%fused_computation.20 | convolution fusion | flops 8513750528 | bytes 10795040 | tf_op jit(solution)/shard_map/dot_general | solution.py:37
  175.6 3.2 convolution_reduce_fusion
  178.8 20.2 %all-gather.2 = f32[4,1,768]{2,1,0:T(1,128)S(1)} all-gather(f32[1,1,768]{2,1,0:T(1,128)S(1)} %reshape.375), channel_id=1, replica_groups=mesh['tok'=8,'tp'=4] {'tp'}, dimensions={0}, use_global_device_ids=true | all-gather | bytes 15360 | tf_op jit(solution)/shard_map/all_gather | solution.py:195
  200.2 3.6 all-to-all-start.1
  203.8 14.8 %fusion.65 = bf16[1200,768]{1,0:T(8,128)(2,1)} fusion(bf16[4616,768]{1,0:T(8,128)(2,1)} %param.29, s32[4616]{0:T(1024)S(1)} %get-tuple-element.47), kind=kOutput, calls=%fused_computation.100 | convolution fusion | flops 8514672128 | bytes 8951840 | tf_op jit(solution)/shard_map/dot_general | solution.py:37
  218.6 6.6 copy.121
  226.7 2.8 fusion.130
  231.2 10.5 %multiply_convert_fusion = (bf16[1200,3072]{1,0:T(8,128)(2,1)S(1)}, f32[1200,3072]{1,0:T(8,128)}) fusion(f32[3072]{0:T(1024)S(1)} %bitcast.228, bf16[768,3072]{0,1:T(8,128)(2,1)S(1)} %bitcast.209, f32[768]{0:T(1024)S(1)} %get-tuple-element.24, f32[768]{0:T(1024)S(1)} %get-tuple-element.23, f32[1200]{0:T(1024)S(1)} %add_rsqrt_fusion, ...), kind=kOutput, calls=%fused_computation.34 | convolution fusion | flops 5691801600 | bytes 31440960 | tf_op jit(solution)/shard_map/dot_general | solution.py:37
  241.7 8.3 %convolution_convert_fusion = bf16[3072,768]{1,0:T(8,128)(2,1)} fusion(bf16[1200,3072]{1,0:T(8,128)(2,1)S(1)} %get-tuple-element.67, bf16[1200,768]{1,0:T(8,128)(2,1)S(1)} %copy-done.16), kind=kOutput, calls=%fused_computation.65 | convolution fusion | flops 5664669696 | bytes 13934592 | tf_op jit(solution)/shard_map/dot_general | solution.py:41
  250.2 14.4 %convert_reduce_fusion = (f32[3072]{0:T(1024)}, bf16[1200,3072]{1,0:T(8,128)(2,1)S(1)}) fusion(f32[1200,3072]{1,0:T(8,128)} %get-tuple-element.68, bf16[1200,768]{1,0:T(8,128)(2,1)} %fusion.65, bf16[3072,768]{1,0:T(8,128)(2,1)} %all-gather.8.cloned.1.call-done), kind=kOutput, calls=%fused_computation.33 | convolution fusion | flops 5706544128 | bytes 28692480 | tf_op jit(solution)/shard_map/dot_general | solution.py:45
  264.6 13.4 %multiply_reduce_fusion.2 = (f32[768]{0:T(1024)}, f32[1200]{0:T(1024)S(1)}, f32[1200]{0:T(1024)S(1)}, f32[768]{0:T(1024)}, f32[1200,768]{1,0:T(8,128)S(1)}) fusion(f32[1200]{0:T(1024)S(1)} %add_rsqrt_fusion, f32[1200]{0:T(1024)S(1)} %broadcast_multiply_fusion.2, f32[1200,768]{1,0:T(8,128)S(1)} %copy-done.3, bf16[576,768]{1,0:T(8,128)(2,1)S(1)} %bitcast.199, ...), kind=kOutput, calls=%fused_computation.86 | convolution fusion | flops 5673365504 | bytes 20382144 | tf_op jit(solution)/shard_map/dot_general | solution.py:45
  278.0 4.2 fusion.60
  284.8 27.2 %all_to_all.41 = bf16[8,72,768]{2,1,0:T(8,128)(2,1)S(1)} all-to-all(bf16[8,72,768]{2,1,0:T(8,128)(2,1)S(1)} %bitcast.218), channel_id=1, replica_groups=mesh['tok'=8,'tp'=4] {'tok'}, dimensions={0} | all-to-all | bytes 1769472 | tf_op jit(solution)/shard_map/all_to_all | solution.py:179
  317.4 17.7 %all-reduce.4 = f32[768]{0:T(1024)} all-reduce(f32[768]{0:T(1024)} %dynamic-update-slice), channel_id=1, replica_groups=mesh['tok'=8,'tp'=4] {'tp'}, use_global_device_ids=true, to_apply=%add.4 | all-reduce | flops 768 | bytes 6144
  336.6 10.9 %convolution_convert_fusion.1 = bf16[768,3072]{1,0:T(8,128)(2,1)S(1)} fusion(bf16[1200,3072]{1,0:T(8,128)(2,1)} %copy-done.52, f32[768]{0:T(1024)} %copy-done.45, f32[768]{0:T(1024)} %copy-done.34, f32[1200]{0:T(1024)} %copy-done.31, f32[1200]{0:T(1024)S(1)} %broadcast_multiply_fusion.2, f32[1200,768]{1,0:T(8,128)} %copy-done.1, ...), kind=kOutput, calls=%fused_computation.66 | convolution fusion | flops 5672042496 | bytes 16683072 | tf_op jit(solution)/shard_map/dot_general | solution.py:41
  347.5 2.5 copy.186
  350.0 7.7 %fusion.56 = bf16[2432,192]{0,1:T(8,128)(2,1)} fusion(s32[2304]{0:T(1024)} %copy-done.39, s32[2432]{0:T(1024)} %copy-done.41, bf16[192,768]{1,0:T(8,128)(2,1)} %param.22, bf16[1152,768]{1,0:T(8,128)(2,1)} %collective-permute-done.4, bf16[576,768]{1,0:T(8,128)(2,1)S(1)} %collective-permute-done.3, bf16[576,768]{1,0:T(8,128)(2,1)S(1)} %bitcast.214), kind=kOutput, calls=%fused_computation.81 | convolution fusion | flops 2848284672 | bytes 4786688 | tf_op jit(solution)/shard_map/dot_general | solution.py:37
  357.8 2.6 reshape.354
  360.5 6.4 fusion.75
  366.8 8.9 %multiply_reduce_fusion = (f32[8,3,304]{2,1,0:T(4,128)S(1)}, f32[8,3,304,304]{2,3,1,0:T(8,128)}) fusion(f32[8,3,304,304]{2,3,1,0:T(8,128)} %get-tuple-element.66, f32[8,3,304]{2,1,0:T(4,128)S(1)} %copy-done.29, bf16[8,304,1,3,64]{1,0,4,3,2:T(8,128)(2,1)S(1)} %copy-done.18, bf16[8,304,3,64]{1,0,3,2:T(8,128)(2,1)S(1)} %reshape.354), kind=kOutput, calls=%fused_computation.40 | convolution fusion | flops 290548608 | bytes 19670016 | tf_op jit(solution)/shard_map/rqhe,rkhe->rhqk/dot_general | solution.py:235
  375.8 6.1 multiply_convert_fusion.1
  386.1 4.1 copy.131
  390.2 6.7 convert_element_type.200
  396.9 16.6 %fusion.62 = f32[2304,768]{1,0:T(8,128)} fusion(bf16[768,576]{0,1:T(8,128)(2,1)S(1)} %bitcast.192, bf16[2432,576]{0,1:T(8,128)(2,1)} %convert_element_type.200, s32[2304]{0:T(1024)S(1)} %copy-done.40, s32[2432]{0:T(1024)S(1)} %copy-done.42), kind=kOutput, calls=%fused_computation.98 | convolution fusion | flops 8500396032 | bytes 10783232 | tf_op jit(solution)/shard_map/dot_general | solution.py:45
  413.6 3.8 slice.288
  417.8 10.6 %fusion.64 = bf16[1200,768]{1,0:T(8,128)(2,1)S(1)} fusion(bf16[1200,3072]{1,0:T(8,128)(2,1)} %copy-done.54, bf16[3072,768]{1,0:T(8,128)(2,1)} %all-gather.8.cloned.1.call-done, f32[768]{0:T(1024)S(1)} %copy-done.49, f32[1200,768]{1,0:T(8,128)} %copy-done.1, bf16[576,768]{1,0:T(8,128)(2,1)S(1)} %bitcast.202, f32[1200]{0:T(1024)S(1)} %fusion.123), kind=kOutput, calls=%fused_computation.99 | convolution fusion | flops 5667840000 | bytes 18513600 | tf_op jit(solution)/shard_map/dot_general | solution.py:37
  431.0 3.5 all-to-all-start.2
  437.6 10.7 %all-to-all-done.2 = bf16[4,576,192]{1,2,0:T(8,128)(2,1)S(1)} async-done(((bf16[4,576,192]{1,2,0:T(8,128)(2,1)}), bf16[4,576,192]{1,2,0:T(8,128)(2,1)S(1)}, u32[]{:S(2)}, u32[]{:S(2)}) %all-to-all-start.2) | async-done | bytes 884768 | tf_op jit(solution)/shard_map/all_to_all | solution.py:262
  448.2 4.2 all-to-all-start.3
  462.2 4.1 all-to-all-done.3
  466.3 3.5 all-to-all-start.7
  469.8 2.9 copy.125
  472.7 2.7 reshape.351
  475.4 2.9 slice_add_fusion
  483.0 13.4 %fusion.2 = f32[4616,192]{0,1:T(8,128)} fusion(bf16[2496,192]{0,1:T(8,128)(2,1)} %reshape.351, s32[4616]{0:T(1024)S(1)} %copy-done.33), kind=kOutput, calls=%fused_computation.3 | convolution fusion | flops 4435791360 | bytes 4522016 | tf_op jit(solution)/shard_map/dot_general | solution.py:37
  496.5 6.8 collective-permute-done.6
  503.3 2.6 fusion.71
  505.9 4.7 all-to-all-start.5
  510.6 13.9 %fusion.40 = bf16[4616,192]{0,1:T(8,128)(2,1)} fusion(f32[4616,192]{0,1:T(8,128)} %fusion.2, bf16[2304,192]{0,1:T(8,128)(2,1)} %reshape.349, s32[4616]{0:T(1024)S(1)} %copy-done.32), kind=kOutput, calls=%fused_computation.57 | convolution fusion | flops 4096349184 | bytes 6220832 | tf_op jit(solution)/shard_map/dot_general | solution.py:37
  526.2 2.7 reshape.359
  529.0 4.0 fusion.86
  533.2 3.4 convolution_convert_fusion.3
  543.3 3.7 all-to-all-start.6
  547.0 13.5 %fusion.1 = f32[4616,192]{0,1:T(8,128)} fusion(bf16[2496,192]{0,1:T(8,128)(2,1)} %reshape.359, s32[4616]{0:T(1024)S(1)} %copy-done.33), kind=kOutput, calls=%fused_computation.2 | convolution fusion | flops 4435791360 | bytes 4522016 | tf_op jit(solution)/shard_map/dot_general | solution.py:37
  560.7 23.7 %psum.43 = f32[2,192]{1,0:T(2,128)} all-reduce(f32[2,192]{1,0:T(2,128)S(1)} %pad_maximum_fusion.8), channel_id=1, replica_groups=mesh['tok'=8,'tp'=4] {'tok'}, use_global_device_ids=true, to_apply=%region_22.23 | all-reduce | flops 384 | bytes 3072 | tf_op jit(solution)/shard_map/psum | solution.py:277
  584.4 38.3 %psum.45 = f32[11,768]{1,0:T(8,128)S(1)} all-reduce(f32[11,768]{1,0:T(8,128)S(1)} %concatenate.16), channel_id=1, replica_groups=mesh['tok'=8,'tp'=4] {'tok','tp'}, use_global_device_ids=true, to_apply=%region_32.33 | all-reduce | flops 8448 | bytes 67584 | tf_op jit(solution)/shard_map/psum | solution.py:274
  626.1 13.6 %fusion.39 = f32[4616,192]{0,1:T(8,128)} fusion(f32[4616,192]{0,1:T(8,128)} %fusion.1, bf16[2304,192]{0,1:T(8,128)(2,1)S(1)} %reshape.357, s32[4616]{0:T(1024)S(1)} %copy-done.32), kind=kOutput, calls=%fused_computation.56 | convolution fusion | flops 4095462912 | bytes 7993376 | tf_op jit(solution)/shard_map/dot_general | solution.py:37
  639.7 42.5 %all-reduce.8.cloned.1.call-done = (bf16[768,3,192]{0,2,1:T(8,128)(2,1)}, bf16[192,768]{1,0:T(8,128)(2,1)}, bf16[768,768]{1,0:T(8,128)(2,1)}, bf16[768,768]{1,0:T(8,128)(2,1)}) async-done(((bf16[768,3,192]{0,2,1:T(8,128)(2,1)}, bf16[192,768]{1,0:T(8,128)(2,1)}, bf16[768,768]{1,0:T(8,128)(2,1)}, bf16[768,768]{1,0:T(8,128)(2,1)}), (bf16[768,3,192]{0,2,1:T(8,128)(2,1)}, bf16[192,768]{1,0:T(8,128)(2,1)}, ...) | async-done | bytes 3538960 | tf_op jit(solution)/shard_map/psum | solution.py:250
  684.2 2.5 reshape.361
  (269 shorter events, 76.2 us)
Async XLA Ops:
  7.2 99.3 %copy-start = (bf16[768,3,192]{0,2,1:T(8,128)(2,1)S(1)}, bf16[768,3,192]{0,2,1:T(8,128)(2,1)}, u32[]{:S(2)}) copy-start(bf16[768,3,192]{0,2,1:T(8,128)(2,1)} %param.20) | copy-start | bytes 2654212
  7.2 211.4 %all-gather.6.cloned.1.call-start = ((), (), s32[]{:S(2)}) async-start(), calls=%async_computation.12 | async-start | bytes 5898240 | tf_op jit(solution)/shard_map/all_gather | solution.py:112
  8.1 23.2 %copy-start.23 = (f32[768]{0:T(1024)}, f32[768]{0:T(1024)S(1)}, u32[]{:S(2)}) copy-start(f32[768]{0:T(1024)S(1)} %get-tuple-element.21) | copy-start | bytes 9220
  32.1 49.1 %copy-start.51 = (f32[192]{0:T(256)S(1)}, f32[192]{0:T(256)}, u32[]{:S(2)}) copy-start(f32[192]{0:T(256)} %param.23) | copy-start | bytes 2308
  32.1 49.4 %copy-start.50 = (f32[2,192]{1,0:T(2,128)S(1)}, f32[2,192]{1,0:T(2,128)}, u32[]{:S(2)}) copy-start(f32[2,192]{1,0:T(2,128)} %param.21) | copy-start | bytes 4612
  80.6 3.9 collective-permute-start
  80.7 169.5 %all-gather.8.cloned.1.call-start = ((), (), s32[]{:S(2)}) async-start(), calls=%async_computation.13 | async-start | bytes 5898240 | tf_op jit(solution)/shard_map/all_gather | solution.py:113
  81.6 59.8 %copy-start.41 = (s32[2432]{0:T(1024)}, s32[2432]{0:T(1024)S(1)}, u32[]{:S(2)}) copy-start(s32[2432]{0:T(1024)S(1)} %fusion.120) | copy-start | bytes 29188
  89.7 51.7 %copy-start.39 = (s32[2304]{0:T(1024)}, s32[2304]{0:T(1024)S(1)}, u32[]{:S(2)}) copy-start(s32[2304]{0:T(1024)S(1)} %eq.201) | copy-start | bytes 27652
  125.7 8.3 %copy-start.7 = (bf16[8,304,1,3,64]{1,0,4,3,2:T(8,128)(2,1)}, bf16[8,304,1,3,64]{1,0,4,3,2:T(8,128)(2,1)S(1)}, u32[]{:S(2)}) copy-start(bf16[8,304,1,3,64]{1,0,4,3,2:T(8,128)(2,1)S(1)} %get-tuple-element.37) | copy-start | bytes 2801668
  125.7 8.3 %copy-start.10 = (bf16[8,304,1,3,64]{1,0,4,3,2:T(8,128)(2,1)}, bf16[8,304,1,3,64]{1,0,4,3,2:T(8,128)(2,1)S(1)}, u32[]{:S(2)}) copy-start(bf16[8,304,1,3,64]{1,0,4,3,2:T(8,128)(2,1)S(1)} %get-tuple-element.38) | copy-start | bytes 2801668
  134.0 5.8 copy-start.28
  149.8 3.9 collective-permute-start.1
  157.1 42.0 %collective-permute-start.2 = (bf16[576,768]{1,0:T(8,128)(2,1)S(1)}, bf16[576,768]{1,0:T(8,128)(2,1)S(1)}, u32[]{:S(2)}, u32[]{:S(2)}) collective-permute-start(bf16[576,768]{1,0:T(8,128)(2,1)S(1)} %slice.292), channel_id=1, source_target_pairs={{0,2},{1,3},{2,0},{3,1},{4,6},{5,7},{6,4},{7,5},{8,10},{9,11},{10,... | collective-permute-start | bytes 2654216 | tf_op jit(solution)/shard_map/ppermute | solution.py:175
  158.5 15.1 %copy-start.46 = (f32[768]{0:T(1024)S(1)}, f32[768]{0:T(1024)}, u32[]{:S(2)}) copy-start(f32[768]{0:T(1024)} %param.26) | copy-start | bytes 9220
  158.5 15.2 %copy-start.35 = (f32[768]{0:T(1024)S(1)}, f32[768]{0:T(1024)}, u32[]{:S(2)}) copy-start(f32[768]{0:T(1024)} %param.18) | copy-start | bytes 9220
  173.6 25.4 %copy-start.44 = (f32[2,768]{1,0:T(2,128)S(1)}, f32[2,768]{1,0:T(2,128)}, u32[]{:S(2)}) copy-start(f32[2,768]{1,0:T(2,128)} %param.24) | copy-start | bytes 18436
  178.8 21.4 %copy-start.25 = (f32[1200]{0:T(1024)}, f32[1200]{0:T(1024)S(1)}, u32[]{:S(2)}) copy-start(f32[1200]{0:T(1024)S(1)} %convolution_reduce_fusion) | copy-start | bytes 14404
  199.0 31.7 %copy-start.45 = (f32[768]{0:T(1024)}, f32[768]{0:T(1024)S(1)}, u32[]{:S(2)}) copy-start(f32[768]{0:T(1024)S(1)} %get-tuple-element.24) | copy-start | bytes 9220
  199.1 78.9 %copy-start.34 = (f32[768]{0:T(1024)}, f32[768]{0:T(1024)S(1)}, u32[]{:S(2)}) copy-start(f32[768]{0:T(1024)S(1)} %get-tuple-element.23) | copy-start | bytes 9220
  200.2 26.5 %all-to-all-start.1 = ((bf16[8,72,768]{2,1,0:T(8,128)(2,1)}), bf16[8,72,768]{2,1,0:T(8,128)(2,1)S(1)}, u32[]{:S(2)}, u32[]{:S(2)}) async-start(bf16[8,72,768]{2,1,0:T(8,128)(2,1)} %bitcast.21), calls=%async_computation.1 | async-start | bytes 1769472 | tf_op jit(solution)/shard_map/all_to_all | solution.py:179
  203.7 335.6 %reduce-scatter.5.cloned.1.call-start = ((), (), s32[]{:S(2)}) async-start(), calls=%async_computation.11 | async-start | bytes 5898240 | tf_op jit(solution)/shard_map/reduce_scatter | solution.py:226
  226.7 4.6 copy-start.9
  230.8 47.2 %copy-start.31 = (f32[1200]{0:T(1024)}, f32[1200]{0:T(1024)S(1)}, u32[]{:S(2)}) copy-start(f32[1200]{0:T(1024)S(1)} %add_rsqrt_fusion) | copy-start | bytes 14404
  231.2 10.5 %copy-start.16 = (bf16[1200,768]{1,0:T(8,128)(2,1)S(1)}, bf16[1200,768]{1,0:T(8,128)(2,1)}, u32[]{:S(2)}) copy-start(bf16[1200,768]{1,0:T(8,128)(2,1)} %fusion.65) | copy-start | bytes 5529604
  241.7 8.3 %copy-start.54 = (bf16[1200,3072]{1,0:T(8,128)(2,1)}, bf16[1200,3072]{1,0:T(8,128)(2,1)S(1)}, u32[]{:S(2)}) copy-start(bf16[1200,3072]{1,0:T(8,128)(2,1)S(1)} %get-tuple-element.67) | copy-start | bytes 22118404
  250.1 289.3 %reduce-scatter.3.cloned.1.call-start = ((), (), s32[]{:S(2)}) async-start(), calls=%async_computation.10 | async-start | bytes 5898240 | tf_op jit(solution)/shard_map/reduce_scatter | solution.py:225
  250.2 14.4 %copy-start.3 = (f32[1200,768]{1,0:T(8,128)S(1)}, f32[1200,768]{1,0:T(8,128)}, u32[]{:S(2)}) copy-start(f32[1200,768]{1,0:T(8,128)} %copy-done.1) | copy-start | bytes 11059204
  264.5 13.4 %copy-start.52 = (bf16[1200,3072]{1,0:T(8,128)(2,1)}, bf16[1200,3072]{1,0:T(8,128)(2,1)S(1)}, u32[]{:S(2)}) copy-start(bf16[1200,3072]{1,0:T(8,128)(2,1)S(1)} %get-tuple-element.73) | copy-start | bytes 22118404
  264.6 13.5 %copy-start.17 = (bf16[1200,768]{1,0:T(8,128)(2,1)S(1)}, bf16[1200,768]{1,0:T(8,128)(2,1)}, u32[]{:S(2)}) copy-start(bf16[1200,768]{1,0:T(8,128)(2,1)} %fusion.65) | copy-start | bytes 5529604
  312.0 38.1 %copy-start.13 = (bf16[8,72,768]{2,1,0:T(8,128)(2,1)}, bf16[8,72,768]{2,1,0:T(8,128)(2,1)S(1)}, u32[]{:S(2)}) copy-start(bf16[8,72,768]{2,1,0:T(8,128)(2,1)S(1)} %all_to_all.41) | copy-start | bytes 2654212
  312.0 23.2 %collective-permute-start.3 = (bf16[576,768]{1,0:T(8,128)(2,1)S(1)}, bf16[576,768]{1,0:T(8,128)(2,1)S(1)}, u32[]{:S(2)}, u32[]{:S(2)}) collective-permute-start(bf16[576,768]{1,0:T(8,128)(2,1)S(1)} %bitcast.212), channel_id=1, source_target_pairs={{0,2},{1,3},{2,0},{3,1},{4,6},{5,7},{6,4},{7,5},{8,10},{9,11},{10,... | collective-permute-start | bytes 2654216 | tf_op jit(solution)/shard_map/ppermute | solution.py:230
  335.2 14.9 %copy-start.21 = (bf16[576,768]{1,0:T(8,128)(2,1)}, bf16[576,768]{1,0:T(8,128)(2,1)S(1)}, u32[]{:S(2)}) copy-start(bf16[576,768]{1,0:T(8,128)(2,1)S(1)} %collective-permute-done.3) | copy-start | bytes 2654212
  336.6 13.4 %collective-permute-start.4 = (bf16[1152,768]{1,0:T(8,128)(2,1)}, bf16[1152,768]{1,0:T(8,128)(2,1)}, u32[]{:S(2)}, u32[]{:S(2)}) collective-permute-start(bf16[1152,768]{1,0:T(8,128)(2,1)} %pad_maximum_fusion.2), channel_id=1, source_target_pairs={{0,1},{1,0},{2,3},{3,2},{4,5},{5,4},{6,7},{7,6},{8,9},{9,8},{10,11... | collective-permute-start | bytes 5308424 | tf_op jit(solution)/shard_map/ppermute | solution.py:231
  360.4 6.4 copy-start.18
  360.4 6.4 copy-start.29
  360.4 15.3 %slice-start = ((s8[11206656]{0:T(1024)(128)(4,1)}), s8[4194304]{0:T(1024)(128)(4,1)S(1)}, s32[]{:S(2)}) async-start(s8[11206656]{0:T(1024)(128)(4,1)} %bitcast.203), calls=%async_computation.15 | async-start | bytes 8388608
  360.4 15.3 %slice-start.1 = ((s8[11206656]{0:T(1024)(128)(4,1)}), s8[4194304]{0:T(1024)(128)(4,1)S(1)}, s32[]{:S(2)}) async-start(s8[11206656]{0:T(1024)(128)(4,1)} %bitcast.203), calls=%async_computation.16 | async-start | bytes 8388608
  366.8 8.9 %slice-start.2 = ((s8[11206656]{0:T(1024)(128)(4,1)}), s8[2818048]{0:T(1024)(128)(4,1)S(1)}, s32[]{:S(2)}) async-start(s8[11206656]{0:T(1024)(128)(4,1)} %bitcast.203), calls=%async_computation.17 | async-start | bytes 5636096
  375.7 6.2 copy-start.11
  390.2 6.7 copy-start.40
  390.2 6.7 copy-start.42
  396.9 20.9 %copy-start.49 = (f32[768]{0:T(1024)S(1)}, f32[768]{0:T(1024)}, u32[]{:S(2)}) copy-start(f32[768]{0:T(1024)} %all-reduce.4) | copy-start | bytes 9220
  417.3 58.1 %collective-permute-start.5 = (bf16[1152,768]{1,0:T(8,128)(2,1)}, bf16[1152,768]{1,0:T(8,128)(2,1)}, u32[]{:S(2)}, u32[]{:S(2)}) collective-permute-start(bf16[1152,768]{1,0:T(8,128)(2,1)} %slice.288), channel_id=1, source_target_pairs={{0,1},{1,0},{2,3},{3,2},{4,5},{5,4},{6,7},{7,6},{8,9},{9,8},{10,11... | collective-permute-start | bytes 5308424 | tf_op jit(solution)/shard_map/ppermute | solution.py:173
  429.7 6.5 slice-start.3
  431.0 17.2 %all-to-all-start.2 = ((bf16[4,576,192]{1,2,0:T(8,128)(2,1)}), bf16[4,576,192]{1,2,0:T(8,128)(2,1)S(1)}, u32[]{:S(2)}, u32[]{:S(2)}) async-start(bf16[4,576,192]{1,2,0:T(8,128)(2,1)} %bitcast.29), calls=%async_computation.2 | async-start | bytes 1966080 | tf_op jit(solution)/shard_map/all_to_all | solution.py:262
  436.2 19.8 %copy-start.43 = (f32[3072]{0:T(1024)S(1)}, f32[3072]{0:T(1024)}, u32[]{:S(2)}) copy-start(f32[3072]{0:T(1024)} %get-tuple-element.72) | copy-start | bytes 36868
  436.2 19.8 %copy-start.48 = (f32[768]{0:T(1024)S(1)}, f32[768]{0:T(1024)}, u32[]{:S(2)}) copy-start(f32[768]{0:T(1024)} %get-tuple-element.13) | copy-start | bytes 9220
  436.2 19.8 %copy-start.47 = (f32[768]{0:T(1024)S(1)}, f32[768]{0:T(1024)}, u32[]{:S(2)}) copy-start(f32[768]{0:T(1024)} %get-tuple-element.18) | copy-start | bytes 9220
  436.2 19.8 %copy-start.38 = (f32[768]{0:T(1024)S(1)}, f32[768]{0:T(1024)}, u32[]{:S(2)}) copy-start(f32[768]{0:T(1024)} %get-tuple-element.40) | copy-start | bytes 9220
  436.2 19.8 %copy-start.26 = (f32[1200]{0:T(1024)S(1)}, f32[1200]{0:T(1024)}, u32[]{:S(2)}) copy-start(f32[1200]{0:T(1024)} %copy-done.25) | copy-start | bytes 14404
  436.2 19.8 %copy-start.30 = (f32[1200]{0:T(1024)S(1)}, f32[1200]{0:T(1024)}, u32[]{:S(2)}) copy-start(f32[1200]{0:T(1024)} %get-tuple-element.33) | copy-start | bytes 14404
  448.2 18.1 %all-to-all-start.3 = ((bf16[4,624,192]{1,2,0:T(8,128)(2,1)}), bf16[4,624,192]{1,2,0:T(8,128)(2,1)}, u32[]{:S(2)}, u32[]{:S(2)}) async-start(bf16[4,624,192]{1,2,0:T(8,128)(2,1)} %bitcast.31), calls=%async_computation.3 | async-start | bytes 1966080 | tf_op jit(solution)/shard_map/all_to_all | solution.py:262
  452.5 6.0 copy-start.37
  456.1 4.5 copy-start.27
  466.3 39.6 %all-to-all-start.7 = ((bf16[4,624,192]{1,2,0:T(8,128)(2,1)}), bf16[4,624,192]{1,2,0:T(8,128)(2,1)S(1)}, u32[]{:S(2)}, u32[]{:S(2)}) async-start(bf16[4,624,192]{1,2,0:T(8,128)(2,1)} %bitcast.211), calls=%async_computation.7 | async-start | bytes 1966080 | tf_op jit(solution)/shard_map/all_to_all | solution.py:262
  475.4 7.6 %copy-start.33 = (s32[4616]{0:T(1024)S(1)}, s32[4616]{0:T(1024)}, u32[]{:S(2)}) copy-start(s32[4616]{0:T(1024)} %get-tuple-element.49) | copy-start | bytes 55396
  481.1 22.2 %collective-permute-start.6 = (bf16[576,768]{1,0:T(8,128)(2,1)}, bf16[576,768]{1,0:T(8,128)(2,1)S(1)}, u32[]{:S(2)}, u32[]{:S(2)}) collective-permute-start(bf16[576,768]{1,0:T(8,128)(2,1)} %slice.291), channel_id=1, source_target_pairs={{0,2},{1,3},{2,0},{3,1},{4,6},{5,7},{6,4},{7,5},{8,10},{9,11},{10,... | collective-permute-start | bytes 2654216 | tf_op jit(solution)/shard_map/ppermute | solution.py:175
  496.5 14.1 %copy-start.32 = (s32[4616]{0:T(1024)S(1)}, s32[4616]{0:T(1024)}, u32[]{:S(2)}) copy-start(s32[4616]{0:T(1024)} %get-tuple-element.45) | copy-start | bytes 55396
  505.9 30.6 %all-to-all-start.5 = ((bf16[8,72,768]{2,1,0:T(8,128)(2,1)}), bf16[8,72,768]{2,1,0:T(8,128)(2,1)S(1)}, u32[]{:S(2)}, u32[]{:S(2)}) async-start(bf16[8,72,768]{2,1,0:T(8,128)(2,1)} %bitcast.216), calls=%async_computation.5 | async-start | bytes 1769472 | tf_op jit(solution)/shard_map/all_to_all | solution.py:179
  510.6 171.6 %all-reduce.8.cloned.1.call-start = ((), (), s32[]{:S(2)}) async-start(), calls=%async_computation.14 | async-start | bytes 7077888 | tf_op jit(solution)/shard_map/psum | solution.py:250
  543.3 81.4 %all-to-all-start.6 = ((bf16[4,576,192]{1,2,0:T(8,128)(2,1)}), bf16[4,576,192]{1,2,0:T(8,128)(2,1)S(1)}, u32[]{:S(2)}, u32[]{:S(2)}) async-start(bf16[4,576,192]{1,2,0:T(8,128)(2,1)} %bitcast.43), calls=%async_computation.6 | async-start | bytes 1966080 | tf_op jit(solution)/shard_map/all_to_all | solution.py:262
  682.2 4.5 copy-start.20
  682.2 6.1 copy-start.19
  (14 other events, 36.3 us)
Sparse Core Ops, SparseCore 0:
  80.8 36.5 all-gather.5
  150.1 55.4 all-gather.7
  250.2 47.7 reduce-scatter.4
  350.1 46.8 reduce-scatter.2
  539.5 142.6 all-reduce.7
where the time goes:
time: 705 us; the launch traced here: 697 us
  matrix products  260 us (37%)
  blocking collectives  175 us (25%)
  local copies, waits for them, and re-layouts  80 us (11%)
  waiting for transfers between devices  72.2 us (10%)
  other arithmetic  63.8 us (9%)
  starting transfers between devices  29.5 us (4%)
  between operations  16.1 us (2%)
    dot_general x14, matrix products, mul(): lax.dot_general(left, right, (((1,), (0,)), ((), ())), preferred_element_...  149 us
    all_to_all x1, blocking collectives, body(): lax.all_to_all(send_rows.reshape(peers, 2, block, width), 'tok', split_ax...  48.4 us
    dot_general x3, matrix products, mul_t1(): lax.dot_general(left, right, (((1,), (1,)), ((), ())), preferred_element_...  44.5 us
    psum x1, waiting for transfers between devices, body(): d_qkv_total = lax.psum(d_qkv_weight.astype(BF), 'tok').astype(F32)  42.5 us
    psum x1, blocking collectives, body(): small = lax.psum(jnp.concatenate([small, first_pair]), ('tok', 'tp'))  38.3 us
    dot_general x5, matrix products, mul_t0(): lax.dot_general(left, right, (((0,), (0,)), ((), ())), preferred_element_...  30.6 us
    all_to_all x1, blocking collectives, across(): lax.all_to_all(rows.reshape(peers, block, width), 'tok', split_axis=0, co...  27.2 us
    psum x1, blocking collectives, body(): d_qv_bias = lax.psum(d_qv_bias, 'tok')  23.7 us
  transfers between devices with their start and end apart: 18, of which 7 were waited for; matrix products, arithmetic and copies ran while one was open for 52% of the time, Pallas kernels for 0%

commit v1 on v0

--- a/solution.py
+++ b/solution.py
@@ -271,7 +271,7 @@
     ).astype(BF)
     d_tokens = mul(picked_hot, to_columns(d_picked)) + mul(idle_hot, to_columns(d_idle))
     first_pair = jnp.stack([jnp.sum(d_normed * first_hat, axis=0), jnp.sum(d_normed, axis=0)])
-    small = lax.psum(jnp.concatenate([small, first_pair]), ("tok", "tp"))
+    small = lax.psum(lax.psum(jnp.concatenate([small, first_pair]), "tp"), "tok")
     small_cols = columns_of(small[shares:], part, shares)
     d_up_bias = lax.dynamic_slice_in_dim(small, part, 1, 0).reshape(width)
     d_qv_bias = lax.psum(d_qv_bias, "tok")

time: 705 us -> 771 us (1.094)
  waiting for transfers between devices: 72.2 us -> 154 us
  blocking collectives: 175 us -> 153 us
  matrix products: 260 us -> 250 us
  local copies, waits for them, and re-layouts: 80 us -> 88.6 us
    psum x1, waiting for transfers between devices: 42.5 us -> 98.8 us  [body(): d_qkv_total = lax.psum(d_qkv_weight.astype(BF), 'tok').astype(F32)]
    psum x1 -> x0, blocking collectives: 38.3 us -> none  [body(): small = lax.psum(jnp.concatenate([small, first_pair]), ('tok', 'tp'))]
    ppermute x2, waiting for transfers between devices: 6.8 us -> 27.5 us  [share_sum(): got_pair = lax.ppermute(joined[picked:].astype(BF), 'tp', pair_swap)]
    ppermute x1, waiting for transfers between devices: 0.01 us -> 18.4 us  [body(): lax.ppermute(grad_own, 'tp', pair_swap)]
    all_to_all x4, waiting for transfers between devices: 14.8 us -> 0.01 us  [to_columns(): lax.all_to_all(pieces, 'tp', split_axis=0, concat_axis=0, tiled=True)]
    psum x1, blocking collectives: 23.7 us -> 37.6 us  [body(): d_qv_bias = lax.psum(d_qv_bias, 'tok')]
  transfers between devices with their start and end apart: 18 -> 18, of which waited for: 7 -> 7; matrix products, arithmetic and copies ran while one was open for 52% -> 44% of each run, Pallas kernels for 0% -> 0%
where the time goes in v1:
time: 771 us; the launch traced here: 763 us
  matrix products  250 us (32%)
  waiting for transfers between devices  154 us (20%)
  blocking collectives  153 us (20%)
  local copies, waits for them, and re-layouts  88.6 us (11%)
  other arithmetic  70.8 us (9%)
  starting transfers between devices  29.5 us (4%)
  between operations  16.3 us (2%)
    dot_general x14, matrix products, mul(): lax.dot_general(left, right, (((1,), (0,)), ((), ())), preferred_element_...  150 us
    psum x1, waiting for transfers between devices, body(): d_qkv_total = lax.psum(d_qkv_weight.astype(BF), 'tok').astype(F32)  98.8 us
    all_to_all x1, blocking collectives, body(): lax.all_to_all(send_rows.reshape(peers, 2, block, width), 'tok', split_ax...  48.4 us
    dot_general x3, matrix products, mul_t1(): lax.dot_general(left, right, (((1,), (1,)), ((), ())), preferred_element_...  38.5 us
    psum x1, blocking collectives, body(): d_qv_bias = lax.psum(d_qv_bias, 'tok')  37.6 us
    dot_general x5, matrix products, mul_t0(): lax.dot_general(left, right, (((0,), (0,)), ((), ())), preferred_element_...  33 us
    ppermute x2, waiting for transfers between devices, share_sum(): got_pair = lax.ppermute(joined[picked:].astype(BF), 'tp', pair_swap)  27.5 us
    all_to_all x1, blocking collectives, across(): lax.all_to_all(rows.reshape(peers, block, width), 'tok', split_axis=0, co...  27 us
  transfers between devices with their start and end apart: 18, of which 7 were waited for; matrix products, arithmetic and copies ran while one was open for 44% of the time, Pallas kernels for 0%

profile of v1, /device:TPU:0, one launch (start us, length us, event | category | flops | bytes accessed | tf_op | source)
XLA Modules:
  0.0 762.6 jit_solution(13293473123180835096)
XLA Ops:
  13.4 14.7 %fusion.135 = (f32[1152]{0:T(1024)S(1)}, f32[1152,768]{1,0:T(8,128)S(1)}) fusion(bf16[4616,768]{1,0:T(8,128)(2,1)} %param.15, s32[4616]{0:T(1024)S(1)} %get-tuple-element.50), kind=kOutput, calls=%fused_computation.269 | convolution fusion | flops 8174084096 | bytes 10652192 | tf_op jit(solution)/shard_map/dot_general | solution.py:37
  31.6 2.6 add_convert_fusion.2
  34.5 48.4 %all_to_all.40 = bf16[8,2,72,768]{3,2,1,0:T(8,128)(2,1)S(1)} all-to-all(bf16[8,2,72,768]{3,2,1,0:T(8,128)(2,1)S(1)} %broadcast_select_fusion), channel_id=1, replica_groups=mesh['tok'=8,'tp'=4] {'tok'}, dimensions={0} | all-to-all | bytes 3538944 | tf_op jit(solution)/shard_map/all_to_all | solution.py:130
  83.7 3.1 collective-permute-done
  88.0 3.9 pad_maximum_fusion
  92.1 12.9 %fusion.44 = bf16[2432,768]{1,0:T(8,128)(2,1)} fusion(bf16[2304,768]{1,0:T(8,128)(2,1)} %bitcast.219, s32[2304]{0:T(1024)S(1)} %eq.201, s32[2432]{0:T(1024)S(1)} %fusion.120), kind=kOutput, calls=%fused_computation.64 | convolution fusion | flops 8614182912 | bytes 7293440 | tf_op jit(solution)/shard_map/dot_general | solution.py:37
  105.0 3.8 select_reduce_fusion
  108.9 6.1 add_convert_fusion
  115.0 7.7 %reshape.344 = bf16[8,304,3,3,64]{1,0,4,3,2:T(8,128)(2,1)} reshape(bf16[2432,576]{0,1:T(8,128)(2,1)} %add_convert_fusion) | data formatting | bytes 5603328 | tf_op jit(solution)/shard_map/reshape | solution.py:155
  124.8 3.4 fusion.131
  128.2 8.3 %fusion.136 = (f32[8,3,304]{2,1,0:T(4,128)S(1)}, f32[8,3,304,304]{2,3,1,0:T(8,128)}) fusion(pred[8,304,304]{1,2,0:T(8,128)(4,1)} %compare_and_fusion, bf16[8,304,1,3,64]{1,0,4,3,2:T(8,128)(2,1)S(1)} %get-tuple-element.42, bf16[8,304,1,3,64]{1,0,4,3,2:T(8,128)(2,1)S(1)} %get-tuple-element.41), kind=kOutput, calls=%fused_computation.270 | convolution fusion | flops 292774176 | bytes 11508224 | tf_op jit(solution)/shard_map/sub | solution.py:161
  136.6 5.8 fusion.83
  144.0 4.1 fusion.53
  149.3 2.9 copy-done.4
  152.4 3.8 collective-permute-done.1
  156.2 3.3 slice_add_fusion.1
  160.9 15.1 %fusion.16 = f32[1200,768]{1,0:T(8,128)S(1)} fusion(bf16[4616,768]{1,0:T(8,128)(2,1)} %param.15, s32[4616]{0:T(1024)S(1)} %get-tuple-element.51), kind=kOutput, calls=%fused_computation.20 | convolution fusion | flops 8513750528 | bytes 10795040 | tf_op jit(solution)/shard_map/dot_general | solution.py:37
  177.8 3.2 convolution_reduce_fusion
  181.1 20.4 %all-gather.2 = f32[4,1,768]{2,1,0:T(1,128)S(1)} all-gather(f32[1,1,768]{2,1,0:T(1,128)S(1)} %reshape.375), channel_id=1, replica_groups=mesh['tok'=8,'tp'=4] {'tp'}, dimensions={0}, use_global_device_ids=true | all-gather | bytes 15360 | tf_op jit(solution)/shard_map/all_gather | solution.py:195
  202.7 3.6 all-to-all-start.1
  206.3 14.7 %fusion.65 = bf16[1200,768]{1,0:T(8,128)(2,1)} fusion(bf16[4616,768]{1,0:T(8,128)(2,1)} %param.29, s32[4616]{0:T(1024)S(1)} %get-tuple-element.51), kind=kOutput, calls=%fused_computation.100 | convolution fusion | flops 8514672128 | bytes 8951840 | tf_op jit(solution)/shard_map/dot_general | solution.py:37
  220.9 6.7 copy.121
  229.2 2.8 fusion.130
  233.7 13.2 %multiply_convert_fusion = (bf16[1200,3072]{1,0:T(8,128)(2,1)}, f32[1200,3072]{1,0:T(8,128)}) fusion(f32[3072]{0:T(1024)S(1)} %bitcast.230, bf16[768,3072]{0,1:T(8,128)(2,1)S(1)} %bitcast.208, f32[768]{0:T(1024)S(1)} %get-tuple-element.24, f32[768]{0:T(1024)S(1)} %get-tuple-element.23, f32[1200]{0:T(1024)S(1)} %add_rsqrt_fusion, ...), kind=kOutput, calls=%fused_computation.34 | convolution fusion | flops 5691801600 | bytes 31440960 | tf_op jit(solution)/shard_map/dot_general | solution.py:37
  247.0 14.0 %convert_reduce_fusion = (f32[3072]{0:T(1024)}, bf16[1200,3072]{1,0:T(8,128)(2,1)S(1)}) fusion(f32[1200,3072]{1,0:T(8,128)} %get-tuple-element.72, bf16[1200,768]{1,0:T(8,128)(2,1)} %fusion.65, bf16[3072,768]{1,0:T(8,128)(2,1)} %all-gather.8.cloned.1.call-done), kind=kOutput, calls=%fused_computation.33 | convolution fusion | flops 5706544128 | bytes 28692480 | tf_op jit(solution)/shard_map/dot_general | solution.py:45
  261.0 7.9 %multiply_reduce_fusion.2 = (f32[768]{0:T(1024)}, f32[1200]{0:T(1024)S(1)}, f32[1200]{0:T(1024)S(1)}, f32[768]{0:T(1024)}, f32[1200,768]{1,0:T(8,128)S(1)}) fusion(f32[1200]{0:T(1024)S(1)} %add_rsqrt_fusion, f32[1200]{0:T(1024)S(1)} %broadcast_multiply_fusion.2, f32[1200,768]{1,0:T(8,128)S(1)} %copy-done.3, bf16[576,768]{1,0:T(8,128)(2,1)S(1)} %bitcast.199, ...), kind=kOutput, calls=%fused_computation.86 | convolution fusion | flops 5673365504 | bytes 20382144 | tf_op jit(solution)/shard_map/dot_general | solution.py:45
  268.9 4.2 fusion.60
  274.1 27.0 %all_to_all.41 = bf16[8,72,768]{2,1,0:T(8,128)(2,1)S(1)} all-to-all(bf16[8,72,768]{2,1,0:T(8,128)(2,1)S(1)} %bitcast.220), channel_id=1, replica_groups=mesh['tok'=8,'tp'=4] {'tok'}, dimensions={0} | all-to-all | bytes 1769472 | tf_op jit(solution)/shard_map/all_to_all | solution.py:179
  302.5 18.4 %collective-permute-done.3 = bf16[576,768]{1,0:T(8,128)(2,1)S(1)} collective-permute-done((bf16[576,768]{1,0:T(8,128)(2,1)S(1)}, bf16[576,768]{1,0:T(8,128)(2,1)S(1)}, u32[]{:S(2)}, u32[]{:S(2)}) %collective-permute-start.3) | collective-permute-done | bytes 884768 | tf_op jit(solution)/shard_map/ppermute | solution.py:230
  322.4 8.1 %convolution_convert_fusion.1 = bf16[768,3072]{1,0:T(8,128)(2,1)S(1)} fusion(bf16[1200,3072]{1,0:T(8,128)(2,1)S(1)} %get-tuple-element.74, f32[768]{0:T(1024)S(1)} %copy-done.61, f32[768]{0:T(1024)S(1)} %copy-done.42, f32[1200]{0:T(1024)S(1)} %copy-done.35, f32[1200]{0:T(1024)S(1)} %broadcast_multiply_fusion.2, f32[1200,768]{1,0:T(8,128)S(1)} %copy-done.3, ...), kind=kOutput, calls=%fused_computation.66 | convolution fusion | flops 5672042496 | bytes 16683072 | tf_op jit(solution)/shard_map/dot_general | solution.py:41
  330.5 2.5 copy.186
  333.3 7.7 %fusion.56 = bf16[2432,192]{0,1:T(8,128)(2,1)} fusion(s32[2304]{0:T(1024)} %copy-done.47, s32[2432]{0:T(1024)} %copy-done.49, bf16[192,768]{1,0:T(8,128)(2,1)} %param.22, bf16[1152,768]{1,0:T(8,128)(2,1)} %collective-permute-done.4, bf16[576,768]{1,0:T(8,128)(2,1)S(1)} %collective-permute-done.3, bf16[576,768]{1,0:T(8,128)(2,1)S(1)} %bitcast.217), kind=kOutput, calls=%fused_computation.81 | convolution fusion | flops 2848284672 | bytes 4786688 | tf_op jit(solution)/shard_map/dot_general | solution.py:37
  341.0 3.5 reshape.354
  344.5 7.0 multiply_reduce_fusion
  351.5 7.2 multiply_convert_fusion.1
  365.6 4.1 copy.131
  369.7 6.7 convert_element_type.200
  376.4 16.6 %fusion.62 = f32[2304,768]{1,0:T(8,128)} fusion(bf16[768,576]{0,1:T(8,128)(2,1)S(1)} %bitcast.192, bf16[2432,576]{0,1:T(8,128)(2,1)} %convert_element_type.200, s32[2304]{0:T(1024)S(1)} %copy-done.48, s32[2432]{0:T(1024)S(1)} %copy-done.50), kind=kOutput, calls=%fused_computation.98 | convolution fusion | flops 8500396032 | bytes 10783232 | tf_op jit(solution)/shard_map/dot_general | solution.py:45
  393.0 3.8 slice.288
  397.1 10.6 %convolution_convert_fusion = bf16[3072,768]{1,0:T(8,128)(2,1)} fusion(bf16[1200,3072]{1,0:T(8,128)(2,1)} %get-tuple-element.71, bf16[1200,768]{1,0:T(8,128)(2,1)} %fusion.65), kind=kOutput, calls=%fused_computation.65 | convolution fusion | flops 5664669696 | bytes 13934592 | tf_op jit(solution)/shard_map/dot_general | solution.py:41
  410.0 2.6 slice.290
  415.0 4.3 all-to-all-start.7
  419.4 2.9 slice_add_fusion
  426.2 2.9 multiply_reduce_fusion.8
  442.2 2.9 copy.135
  445.2 2.7 reshape.359
  447.9 27.5 %collective-permute-done.6 = bf16[576,768]{1,0:T(8,128)(2,1)S(1)} collective-permute-done((bf16[576,768]{1,0:T(8,128)(2,1)S(1)}, bf16[576,768]{1,0:T(8,128)(2,1)S(1)}, u32[]{:S(2)}, u32[]{:S(2)}) %collective-permute-start.6) | collective-permute-done | bytes 884768 | tf_op jit(solution)/shard_map/ppermute | solution.py:175
  475.3 2.6 fusion.71
  477.9 3.7 all-to-all-start.5
  481.7 13.4 %fusion.1 = f32[4616,192]{0,1:T(8,128)} fusion(bf16[2496,192]{0,1:T(8,128)(2,1)} %reshape.359, s32[4616]{0:T(1024)S(1)} %copy-done.37), kind=kOutput, calls=%fused_computation.2 | convolution fusion | flops 4435791360 | bytes 4522016 | tf_op jit(solution)/shard_map/dot_general | solution.py:37
  496.4 6.3 convolution_convert_fusion.3
  507.9 2.5 add_convert_fusion.3
  511.8 4.2 all-to-all-start.6
  516.2 19.9 %all-reduce.6 = (f32[768]{0:T(1024)S(1)}, f32[11,768]{1,0:T(8,128)S(1)}) all-reduce(f32[768]{0:T(1024)S(1)} %copy-done.46, f32[11,768]{1,0:T(8,128)S(1)} %concatenate.16), channel_id=1, replica_groups=mesh['tok'=8,'tp'=4] {'tp'}, use_global_device_ids=true, to_apply=%add.4 | all-reduce | flops 9216 | bytes 73728
  536.1 10.6 %fusion.64 = bf16[1200,768]{1,0:T(8,128)(2,1)S(1)} fusion(bf16[1200,3072]{1,0:T(8,128)(2,1)} %get-tuple-element.71, bf16[3072,768]{1,0:T(8,128)(2,1)} %all-gather.8.cloned.1.call-done, f32[768]{0:T(1024)S(1)} %get-tuple-element.27, f32[1200,768]{1,0:T(8,128)} %copy-done.1, bf16[576,768]{1,0:T(8,128)(2,1)S(1)} %bitcast.202, f32[1200]{0:T(1024)S(1)} %fusion.123), kind=kOutput, calls=%fused_computation.99 | convolution fusion | flops 5667840000 | bytes 18513600 | tf_op jit(solution)/shard_map/dot_general | solution.py:37
  549.4 3.5 all-to-all-start.2
  552.9 3.9 fusion.86
  556.8 37.6 %all-reduce.5 = (f32[2,192]{1,0:T(2,128)}, f32[11,768]{1,0:T(8,128)S(1)}) all-reduce(f32[2,192]{1,0:T(2,128)S(1)} %pad_maximum_fusion.8, f32[11,768]{1,0:T(8,128)S(1)} %get-tuple-element.28), channel_id=1, replica_groups=mesh['tok'=8,'tp'=4] {'tok'}, use_global_device_ids=true, to_apply=%region_22.23 | all-reduce | flops 8832 | bytes 70656 | tf_op jit(solution)/shard_map/psum | solution.py:277
  601.3 4.2 all-to-all-start.3
  608.0 13.7 %fusion.39 = f32[4616,192]{0,1:T(8,128)} fusion(f32[4616,192]{0,1:T(8,128)} %fusion.1, bf16[2304,192]{0,1:T(8,128)(2,1)} %reshape.357, s32[4616]{0:T(1024)S(1)} %copy-done.36), kind=kOutput, calls=%fused_computation.56 | convolution fusion | flops 4095462912 | bytes 7993376 | tf_op jit(solution)/shard_map/dot_general | solution.py:37
  624.4 12.1 %fusion.2 = f32[4616,192]{0,1:T(8,128)} fusion(bf16[2496,192]{0,1:T(8,128)(2,1)S(1)} %reshape.351, s32[4616]{0:T(1024)S(1)} %copy-done.38), kind=kOutput, calls=%fused_computation.3 | convolution fusion | flops 4435791360 | bytes 4522016 | tf_op jit(solution)/shard_map/dot_general | solution.py:37
  636.5 13.5 %fusion.40 = bf16[4616,192]{0,1:T(8,128)(2,1)} fusion(f32[4616,192]{0,1:T(8,128)} %fusion.2, bf16[2304,192]{0,1:T(8,128)(2,1)S(1)} %copy-done.20, s32[4616]{0:T(1024)S(1)} %copy-done.36), kind=kOutput, calls=%fused_computation.57 | convolution fusion | flops 4096349184 | bytes 6220832 | tf_op jit(solution)/shard_map/dot_general | solution.py:37
  650.0 98.8 %all-reduce.10.cloned.1.call-done = (bf16[768,3,192]{0,2,1:T(8,128)(2,1)}, bf16[192,768]{1,0:T(8,128)(2,1)}, bf16[768,768]{1,0:T(8,128)(2,1)}, bf16[768,768]{1,0:T(8,128)(2,1)}) async-done(((bf16[768,3,192]{0,2,1:T(8,128)(2,1)}, bf16[192,768]{1,0:T(8,128)(2,1)}, bf16[768,768]{1,0:T(8,128)(2,1)}, bf16[768,768]{1,0:T(8,128)(2,1)}), (bf16[768,3,192]{0,2,1:T(8,128)(2,1)}, bf16[192,768]{1,0:T(8,128)(2,1)}, ...) | async-done | bytes 3538960 | tf_op jit(solution)/shard_map/psum | solution.py:250
  748.8 3.0 convert_element_type.216
  (300 shorter events, 83.3 us)
Async XLA Ops:
  7.2 101.7 %copy-start = (bf16[768,3,192]{0,2,1:T(8,128)(2,1)S(1)}, bf16[768,3,192]{0,2,1:T(8,128)(2,1)}, u32[]{:S(2)}) copy-start(bf16[768,3,192]{0,2,1:T(8,128)(2,1)} %param.20) | copy-start | bytes 2654212
  7.2 213.7 %all-gather.6.cloned.1.call-start = ((), (), s32[]{:S(2)}) async-start(), calls=%async_computation.12 | async-start | bytes 5898240 | tf_op jit(solution)/shard_map/all_gather | solution.py:112
  13.4 17.0 %copy-start.58 = (f32[2,768]{1,0:T(2,128)S(1)}, f32[2,768]{1,0:T(2,128)}, u32[]{:S(2)}) copy-start(f32[2,768]{1,0:T(2,128)} %param.19) | copy-start | bytes 18436
  34.4 48.9 %copy-start.68 = (f32[192]{0:T(256)S(1)}, f32[192]{0:T(256)}, u32[]{:S(2)}) copy-start(f32[192]{0:T(256)} %param.23) | copy-start | bytes 2308
  34.5 49.1 %copy-start.67 = (f32[2,192]{1,0:T(2,128)S(1)}, f32[2,192]{1,0:T(2,128)}, u32[]{:S(2)}) copy-start(f32[2,192]{1,0:T(2,128)} %param.21) | copy-start | bytes 4612
  82.9 3.9 collective-permute-start
  83.1 163.9 %all-gather.8.cloned.1.call-start = ((), (), s32[]{:S(2)}) async-start(), calls=%async_computation.13 | async-start | bytes 5898240 | tf_op jit(solution)/shard_map/all_gather | solution.py:113
  83.7 60.2 %copy-start.49 = (s32[2432]{0:T(1024)}, s32[2432]{0:T(1024)S(1)}, u32[]{:S(2)}) copy-start(s32[2432]{0:T(1024)S(1)} %fusion.120) | copy-start | bytes 29188
  92.1 51.9 %copy-start.47 = (s32[2304]{0:T(1024)}, s32[2304]{0:T(1024)S(1)}, u32[]{:S(2)}) copy-start(s32[2304]{0:T(1024)S(1)} %eq.201) | copy-start | bytes 27652
  128.2 8.3 %copy-start.8 = (bf16[8,304,1,3,64]{1,0,4,3,2:T(8,128)(2,1)}, bf16[8,304,1,3,64]{1,0,4,3,2:T(8,128)(2,1)S(1)}, u32[]{:S(2)}) copy-start(bf16[8,304,1,3,64]{1,0,4,3,2:T(8,128)(2,1)S(1)} %get-tuple-element.41) | copy-start | bytes 2801668
  128.2 8.3 %copy-start.11 = (bf16[8,304,1,3,64]{1,0,4,3,2:T(8,128)(2,1)}, bf16[8,304,1,3,64]{1,0,4,3,2:T(8,128)(2,1)S(1)}, u32[]{:S(2)}) copy-start(bf16[8,304,1,3,64]{1,0,4,3,2:T(8,128)(2,1)S(1)} %get-tuple-element.42) | copy-start | bytes 2801668
  136.5 5.8 copy-start.31
  152.3 3.9 collective-permute-start.1
  159.6 42.0 %collective-permute-start.2 = (bf16[576,768]{1,0:T(8,128)(2,1)S(1)}, bf16[576,768]{1,0:T(8,128)(2,1)S(1)}, u32[]{:S(2)}, u32[]{:S(2)}) collective-permute-start(bf16[576,768]{1,0:T(8,128)(2,1)S(1)} %slice.292), channel_id=1, source_target_pairs={{0,2},{1,3},{2,0},{3,1},{4,6},{5,7},{6,4},{7,5},{8,10},{9,11},{10,... | collective-permute-start | bytes 2654216 | tf_op jit(solution)/shard_map/ppermute | solution.py:175
  160.9 15.1 %copy-start.43 = (f32[768]{0:T(1024)S(1)}, f32[768]{0:T(1024)}, u32[]{:S(2)}) copy-start(f32[768]{0:T(1024)} %param.18) | copy-start | bytes 9220
  160.9 15.2 %copy-start.62 = (f32[768]{0:T(1024)S(1)}, f32[768]{0:T(1024)}, u32[]{:S(2)}) copy-start(f32[768]{0:T(1024)} %param.26) | copy-start | bytes 9220
  176.1 25.4 %copy-start.59 = (f32[2,768]{1,0:T(2,128)S(1)}, f32[2,768]{1,0:T(2,128)}, u32[]{:S(2)}) copy-start(f32[2,768]{1,0:T(2,128)} %param.24) | copy-start | bytes 18436
  181.0 21.6 %copy-start.26 = (f32[1200]{0:T(1024)}, f32[1200]{0:T(1024)S(1)}, u32[]{:S(2)}) copy-start(f32[1200]{0:T(1024)S(1)} %convolution_reduce_fusion) | copy-start | bytes 14404
  201.5 31.7 %copy-start.60 = (f32[768]{0:T(1024)}, f32[768]{0:T(1024)S(1)}, u32[]{:S(2)}) copy-start(f32[768]{0:T(1024)S(1)} %get-tuple-element.24) | copy-start | bytes 9220
  201.6 67.3 %copy-start.41 = (f32[768]{0:T(1024)}, f32[768]{0:T(1024)S(1)}, u32[]{:S(2)}) copy-start(f32[768]{0:T(1024)S(1)} %get-tuple-element.23) | copy-start | bytes 9220
  202.7 26.5 %all-to-all-start.1 = ((bf16[8,72,768]{2,1,0:T(8,128)(2,1)}), bf16[8,72,768]{2,1,0:T(8,128)(2,1)S(1)}, u32[]{:S(2)}, u32[]{:S(2)}) async-start(bf16[8,72,768]{2,1,0:T(8,128)(2,1)} %bitcast.21), calls=%async_computation.1 | async-start | bytes 1769472 | tf_op jit(solution)/shard_map/all_to_all | solution.py:179
  206.2 401.7 %reduce-scatter.3.cloned.1.call-start = ((), (), s32[]{:S(2)}) async-start(), calls=%async_computation.10 | async-start | bytes 5898240 | tf_op jit(solution)/shard_map/reduce_scatter | solution.py:225
  233.3 35.6 %copy-start.34 = (f32[1200]{0:T(1024)}, f32[1200]{0:T(1024)S(1)}, u32[]{:S(2)}) copy-start(f32[1200]{0:T(1024)S(1)} %add_rsqrt_fusion) | copy-start | bytes 14404
  233.7 27.2 %slice-start.3 = ((s8[4718592]{0:T(1024)(128)(4,1)}), s8[524288]{0:T(1024)(128)(4,1)S(1)}, s32[]{:S(2)}) async-start(s8[4718592]{0:T(1024)(128)(4,1)} %bitcast.209), calls=%async_computation.18 | async-start | bytes 1048576
  246.9 14.0 %copy-start.3 = (f32[1200,768]{1,0:T(8,128)S(1)}, f32[1200,768]{1,0:T(8,128)}, u32[]{:S(2)}) copy-start(f32[1200,768]{1,0:T(8,128)} %copy-done.1) | copy-start | bytes 11059204
  247.0 14.0 %slice-start.4 = ((s8[4718592]{0:T(1024)(128)(4,1)}), s8[4194304]{0:T(1024)(128)(4,1)S(1)}, s32[]{:S(2)}) async-start(s8[4718592]{0:T(1024)(128)(4,1)} %bitcast.209), calls=%async_computation.19 | async-start | bytes 8388608
  261.0 7.9 %copy-start.16 = (bf16[1200,768]{1,0:T(8,128)(2,1)S(1)}, bf16[1200,768]{1,0:T(8,128)(2,1)}, u32[]{:S(2)}) copy-start(bf16[1200,768]{1,0:T(8,128)(2,1)} %fusion.65) | copy-start | bytes 5529604
  273.1 49.3 %copy-start.5 = (f32[1200,768]{1,0:T(8,128)}, f32[1200,768]{1,0:T(8,128)S(1)}, u32[]{:S(2)}) copy-start(f32[1200,768]{1,0:T(8,128)S(1)} %get-tuple-element.36) | copy-start | bytes 11059204
  273.1 49.3 %copy-start.35 = (f32[1200]{0:T(1024)S(1)}, f32[1200]{0:T(1024)}, u32[]{:S(2)}) copy-start(f32[1200]{0:T(1024)} %copy-done.34) | copy-start | bytes 14404
  273.1 49.3 %copy-start.42 = (f32[768]{0:T(1024)S(1)}, f32[768]{0:T(1024)}, u32[]{:S(2)}) copy-start(f32[768]{0:T(1024)} %copy-done.41) | copy-start | bytes 9220
  273.1 49.3 %copy-start.61 = (f32[768]{0:T(1024)S(1)}, f32[768]{0:T(1024)}, u32[]{:S(2)}) copy-start(f32[768]{0:T(1024)} %copy-done.60) | copy-start | bytes 9220
  301.0 32.2 %copy-start.14 = (bf16[8,72,768]{2,1,0:T(8,128)(2,1)}, bf16[8,72,768]{2,1,0:T(8,128)(2,1)S(1)}, u32[]{:S(2)}) copy-start(bf16[8,72,768]{2,1,0:T(8,128)(2,1)S(1)} %all_to_all.41) | copy-start | bytes 2654212
  301.0 19.9 %collective-permute-start.3 = (bf16[576,768]{1,0:T(8,128)(2,1)S(1)}, bf16[576,768]{1,0:T(8,128)(2,1)S(1)}, u32[]{:S(2)}, u32[]{:S(2)}) collective-permute-start(bf16[576,768]{1,0:T(8,128)(2,1)S(1)} %bitcast.215), channel_id=1, source_target_pairs={{0,2},{1,3},{2,0},{3,1},{4,6},{5,7},{6,4},{7,5},{8,10},{9,11},{10,... | collective-permute-start | bytes 2654216 | tf_op jit(solution)/shard_map/ppermute | solution.py:230
  321.0 12.3 %copy-start.19 = (bf16[576,768]{1,0:T(8,128)(2,1)}, bf16[576,768]{1,0:T(8,128)(2,1)S(1)}, u32[]{:S(2)}) copy-start(bf16[576,768]{1,0:T(8,128)(2,1)S(1)} %collective-permute-done.3) | copy-start | bytes 2654212
  322.4 10.9 %collective-permute-start.4 = (bf16[1152,768]{1,0:T(8,128)(2,1)}, bf16[1152,768]{1,0:T(8,128)(2,1)}, u32[]{:S(2)}, u32[]{:S(2)}) collective-permute-start(bf16[1152,768]{1,0:T(8,128)(2,1)} %pad_maximum_fusion.2), channel_id=1, source_target_pairs={{0,1},{1,0},{2,3},{3,2},{4,5},{5,4},{6,7},{7,6},{8,9},{9,8},{10,11... | collective-permute-start | bytes 5308424 | tf_op jit(solution)/shard_map/ppermute | solution.py:231
  333.0 274.9 %reduce-scatter.5.cloned.1.call-start = ((), (), s32[]{:S(2)}) async-start(), calls=%async_computation.11 | async-start | bytes 5898240 | tf_op jit(solution)/shard_map/reduce_scatter | solution.py:226
  344.5 7.0 copy-start.32
  351.5 7.3 copy-start.9
  351.5 10.5 %slice-start = ((s8[11206656]{0:T(1024)(128)(4,1)}), s8[4194304]{0:T(1024)(128)(4,1)S(1)}, s32[]{:S(2)}) async-start(s8[11206656]{0:T(1024)(128)(4,1)} %bitcast.203), calls=%async_computation.15 | async-start | bytes 8388608
  351.5 10.5 %slice-start.1 = ((s8[11206656]{0:T(1024)(128)(4,1)}), s8[4194304]{0:T(1024)(128)(4,1)S(1)}, s32[]{:S(2)}) async-start(s8[11206656]{0:T(1024)(128)(4,1)} %bitcast.203), calls=%async_computation.16 | async-start | bytes 8388608
  369.7 6.7 copy-start.48
  369.7 6.7 copy-start.50
  396.8 22.6 %collective-permute-start.5 = (bf16[1152,768]{1,0:T(8,128)(2,1)}, bf16[1152,768]{1,0:T(8,128)(2,1)}, u32[]{:S(2)}, u32[]{:S(2)}) collective-permute-start(bf16[1152,768]{1,0:T(8,128)(2,1)} %slice.288), channel_id=1, source_target_pairs={{0,1},{1,0},{2,3},{3,2},{4,5},{5,4},{6,7},{7,6},{8,9},{9,8},{10,11... | collective-permute-start | bytes 5308424 | tf_op jit(solution)/shard_map/ppermute | solution.py:173
  415.0 27.2 %all-to-all-start.7 = ((bf16[4,624,192]{1,2,0:T(8,128)(2,1)}), bf16[4,624,192]{1,2,0:T(8,128)(2,1)}, u32[]{:S(2)}, u32[]{:S(2)}) async-start(bf16[4,624,192]{1,2,0:T(8,128)(2,1)} %bitcast.214), calls=%async_computation.7 | async-start | bytes 1966080 | tf_op jit(solution)/shard_map/all_to_all | solution.py:262
  419.3 6.9 copy-start.28
  419.4 14.9 %copy-start.27 = (f32[1200]{0:T(1024)S(1)}, f32[1200]{0:T(1024)}, u32[]{:S(2)}) copy-start(f32[1200]{0:T(1024)} %copy-done.26) | copy-start | bytes 14404
  424.2 51.1 %collective-permute-start.6 = (bf16[576,768]{1,0:T(8,128)(2,1)S(1)}, bf16[576,768]{1,0:T(8,128)(2,1)S(1)}, u32[]{:S(2)}, u32[]{:S(2)}) collective-permute-start(bf16[576,768]{1,0:T(8,128)(2,1)S(1)} %slice.291), channel_id=1, source_target_pairs={{0,2},{1,3},{2,0},{3,1},{4,6},{5,7},{6,4},{7,5},{8,10},{9,11},{10,... | collective-permute-start | bytes 2654216 | tf_op jit(solution)/shard_map/ppermute | solution.py:175
  433.0 6.2 copy-start.44
  433.0 6.7 copy-start.64
  433.0 7.3 copy-start.63
  475.3 6.3 copy-start.37
  477.9 25.2 %all-to-all-start.5 = ((bf16[8,72,768]{2,1,0:T(8,128)(2,1)}), bf16[8,72,768]{2,1,0:T(8,128)(2,1)S(1)}, u32[]{:S(2)}, u32[]{:S(2)}) async-start(bf16[8,72,768]{2,1,0:T(8,128)(2,1)} %bitcast.40), calls=%async_computation.5 | async-start | bytes 1769472 | tf_op jit(solution)/shard_map/all_to_all | solution.py:179
  481.7 13.5 %copy-start.40 = (f32[3,3,64]{2,1,0:T(4,128)S(1)}, f32[3,3,64]{2,1,0:T(4,128)}, u32[]{:S(2)}) copy-start(f32[3,3,64]{2,1,0:T(4,128)} %get-tuple-element.33) | copy-start | bytes 6916
  496.4 6.7 copy-start.25
  496.4 6.8 copy-start.29
  496.4 6.8 copy-start.33
  510.4 5.7 copy-start.30
  510.5 5.7 copy-start.46
  511.8 37.5 %all-to-all-start.6 = ((bf16[4,576,192]{1,2,0:T(8,128)(2,1)}), bf16[4,576,192]{1,2,0:T(8,128)(2,1)}, u32[]{:S(2)}, u32[]{:S(2)}) async-start(bf16[4,576,192]{1,2,0:T(8,128)(2,1)} %bitcast.213), calls=%async_computation.6 | async-start | bytes 1966080 | tf_op jit(solution)/shard_map/all_to_all | solution.py:262
  549.4 51.9 %all-to-all-start.2 = ((bf16[4,576,192]{1,2,0:T(8,128)(2,1)}), bf16[4,576,192]{1,2,0:T(8,128)(2,1)S(1)}, u32[]{:S(2)}, u32[]{:S(2)}) async-start(bf16[4,576,192]{1,2,0:T(8,128)(2,1)} %bitcast.29), calls=%async_computation.2 | async-start | bytes 1966080 | tf_op jit(solution)/shard_map/all_to_all | solution.py:262
  552.9 41.5 %slice-start.5 = ((bf16[1200,768]{1,0:T(8,128)(2,1)}), bf16[624,768]{1,0:T(8,128)(2,1)S(1)}, s32[]{:S(2)}) async-start(bf16[1200,768]{1,0:T(8,128)(2,1)} %copy-done.13), calls=%async_computation.20 | async-start | bytes 1916928 | tf_op jit(solution)/shard_map/slice | solution.py:270
  601.3 20.4 %all-to-all-start.3 = ((bf16[4,624,192]{1,2,0:T(8,128)(2,1)}), bf16[4,624,192]{1,2,0:T(8,128)(2,1)}, u32[]{:S(2)}, u32[]{:S(2)}) async-start(bf16[4,624,192]{1,2,0:T(8,128)(2,1)} %bitcast.31), calls=%async_computation.3 | async-start | bytes 1966080 | tf_op jit(solution)/shard_map/all_to_all | solution.py:262
  605.5 143.3 %all-reduce.10.cloned.1.call-start = ((), (), s32[]{:S(2)}) async-start(), calls=%async_computation.14 | async-start | bytes 7077888 | tf_op jit(solution)/shard_map/psum | solution.py:250
  624.4 12.1 %copy-start.20 = (bf16[2304,192]{0,1:T(8,128)(2,1)S(1)}, bf16[2304,192]{0,1:T(8,128)(2,1)}, u32[]{:S(2)}) copy-start(bf16[2304,192]{0,1:T(8,128)(2,1)} %reshape.349) | copy-start | bytes 2654212
  (29 other events, 106.1 us)
Sparse Core Ops, SparseCore 0:
  83.2 36.5 all-gather.5
  152.6 55.5 all-gather.7
  333.1 47.8 reduce-scatter.2
  407.9 70.8 reduce-scatter.4
  610.6 138.1 all-reduce.9
